TPU v7x, 256 devices: a whole 4x4x8 slice. The times are simulated.
256 devices in a mesh: term: 4 (over x), sector: 64 (over y, z, core).
Axes of the slice: x: 4, y: 4, z: 8, core: 2. Of those that a mesh axis runs over, the one named last changes fastest.
Arguments:
- psi_blocks: bfloat16 [4096, 128, 128], P('sector'), may hold values from -6 to 6
- right_ops: bfloat16 [8, 4096, 128, 128], P('term', 'sector'), may hold values from -0.5 to 0.5
- left_ops: bfloat16 [8, 4096, 128, 128], P('term', 'sector'), may hold values from -0.1875 to 0.1875
- owner_map: int32 [4096, 1], P('sector'), may hold values from 0 to 63; in each aligned block of 64 rows (0 to 63, 64 to 127, ...) at most 2 rows name the same one
- left_local: int32 [4096, 1], P('sector'), may hold values from 0 to 63
Outputs:
- sigma: bfloat16 [4096, 128, 128], P('sector', 'term')
Inputs may be any that keep to these rules, and one draw needn't show every extreme that they name: `owner_map`: among the 64 sectors held by one device along `sector` (aligned blocks), at most 2 name the same owner; some block reaches it.
All inputs are finite; a program needn't handle non-finite values.
Results may differ from a plain program's by a relative error of at most 0.0049.
Values may be sent and summed in bfloat16 or wider, within the bound.
A program may use at most 128 MiB of HBM per device.

v0:
```python
import jax
import jax.numpy as jnp
from jax import lax
from jax.sharding import PartitionSpec as P


def ranks_of(owners):
    count = owners.shape[-1]
    same = owners[..., :, None] == owners[..., None, :]
    earlier = lax.broadcasted_iota(jnp.int32, (count, count), 0) < lax.broadcasted_iota(
        jnp.int32, (count, count), 1
    )
    return jnp.sum((same & earlier).astype(jnp.int32), axis=-2)


def local(psi_blocks, right_ops, left_ops, owner_map, left_local):
    sec_dev = psi_blocks.shape[0]
    width = psi_blocks.shape[1]
    terms_dev = right_ops.shape[0]
    n_sector = lax.axis_size("sector")
    capacity = max(2, 2 * sec_dev // n_sector)
    slots = n_sector * capacity
    owners = owner_map[:, 0]
    slot_id = owners * capacity + ranks_of(owners)
    packer = (lax.broadcasted_iota(jnp.int32, (slots, sec_dev), 0) == slot_id[None, :]).astype(
        jnp.bfloat16
    )
    routes_all = lax.all_gather(
        jnp.concatenate([owner_map, left_local], axis=1), "sector", axis=0, tiled=True
    )
    all_owners = routes_all[:, 0].reshape(n_sector, sec_dev)
    all_local = routes_all[:, 1].reshape(n_sector, sec_dev)
    all_ranks = ranks_of(all_owners)
    mine = lax.axis_index("sector")
    slot_iota = lax.broadcasted_iota(jnp.int32, (1, 1, capacity), 2)
    hits = (all_owners == mine)[:, :, None] & (all_ranks[:, :, None] == slot_iota)
    tags = (jnp.sum(jnp.where(hits, all_local[:, :, None] + 1, 0), axis=1) - 1).reshape(slots)
    inter = jnp.einsum(
        "sij,tsjk->stik", psi_blocks, right_ops, preferred_element_type=jnp.float32
    ).astype(jnp.bfloat16)
    packed = jnp.dot(packer, inter.reshape(sec_dev, -1), preferred_element_type=jnp.float32).astype(
        jnp.bfloat16
    )
    arrived = lax.all_to_all(
        packed.reshape(n_sector, capacity, -1), "sector", split_axis=0, concat_axis=0, tiled=True
    )
    arrived = arrived.reshape(slots, terms_dev, width, width)
    picked = jnp.take(left_ops, jnp.clip(tags, 0, sec_dev - 1), axis=1)
    images = jnp.einsum("tnij,ntjk->nik", picked, arrived, preferred_element_type=jnp.float32)
    collect = (lax.broadcasted_iota(jnp.int32, (sec_dev, slots), 0) == tags[None, :]).astype(
        jnp.float32
    )
    partial_sum = jnp.dot(
        collect,
        images.reshape(slots, -1),
        precision=lax.Precision.HIGHEST,
        preferred_element_type=jnp.float32,
    ).reshape(sec_dev, width, width)
    total = lax.psum(partial_sum, "term")
    row_count = width // lax.axis_size("term")
    mine_rows = lax.dynamic_slice_in_dim(total, lax.axis_index("term") * row_count, row_count, 1)
    return mine_rows.astype(jnp.bfloat16)


def solution(mesh):
    placed = (
        P("sector", None, None),
        P("term", "sector", None, None),
        P("term", "sector", None, None),
        P("sector", None),
        P("sector", None),
    )
    return jax.shard_map(
        local, mesh=mesh, in_specs=placed, out_specs=P("sector", "term", None), check_vma=False
    )
```

profile of v0, /device:TPU:1, one launch (start us, length us, event | category | flops | bytes accessed | tf_op | source)
XLA Modules:
  0.0 411.3 jit_solution(9655905848802338681)
XLA Ops:
  0.0 0.0 copy-start
  0.0 0.9 convert_reduce_fusion.1
  0.9 0.7 multiply_add_fusion
  1.6 0.0 copy-done
  1.6 5.4 %convert_bitcast_fusion = bf16[64,2,128,128]{2,3,1,0:T(8,128)(2,1)} fusion(bf16[2,64,128,128]{3,2,1,0:T(8,128)(2,1)} %param.6, bf16[64,128,128]{2,1,0:T(8,128)(2,1)S(1)} %copy-done), kind=kOutput, calls=%fused_computation.12 | convolution fusion | flops 538968064 | bytes 10485760 | tf_op jit(solution)/shard_map/sij,tsjk->stik/dot_general | solution.py:38
  7.0 6.3 %copy.23 = bf16[64,2,128,128]{3,2,1,0:T(8,128)(2,1)} copy(bf16[64,2,128,128]{2,3,1,0:T(8,128)(2,1)} %convert_bitcast_fusion) | data formatting | bytes 8388608 | tf_op jit(solution)/shard_map/convert_element_type | solution.py:40
  13.4 8.8 %convolution_convert_fusion = bf16[128,32768]{1,0:T(8,128)(2,1)} fusion(bf16[8,8,256,128]{3,2,1,0:T(8,128)(2,1)} %bitcast.41, s32[64]{0:T(128)S(1)} %multiply_add_fusion), kind=kOutput, calls=%fused_computation.1 | convolution fusion | flops 541073408 | bytes 12583168 | tf_op jit(solution)/shard_map/dot_general | solution.py:41
  22.1 14.1 %reshape.90 = bf16[64,2,32768]{2,1,0:T(2,128)(2,1)} reshape(bf16[128,32768]{1,0:T(8,128)(2,1)} %convolution_convert_fusion) | data formatting | bytes 16777216 | tf_op jit(solution)/shard_map/reshape | solution.py:45
  36.3 13.5 %all-to-all-start = ((bf16[64,2,32768]{2,1,0:T(2,128)(2,1)}), bf16[64,2,32768]{2,1,0:T(2,128)(2,1)}, u32[]{:S(2)}, u32[]{:S(2)}) async-start(bf16[64,2,32768]{2,1,0:T(2,128)(2,1)} %reshape.90), calls=%async_computation | async-start | bytes 16777216 | tf_op jit(solution)/shard_map/all_to_all | solution.py:44
  49.8 0.0 copy-done.2
  49.8 0.0 copy-done.3
  49.8 218.2 %all-gather = s32[64,64,2]{1,2,0:T(2,128)S(1)} all-gather(s32[1,64,2]{1,2,0:T(2,128)S(1)} %add_bitcast_fusion), channel_id=1, replica_groups=mesh['term'=4,'sector'=64] {'sector'}, dimensions={0}, use_global_device_ids=true | all-gather | bytes 33280 | tf_op jit(solution)/shard_map/all_gather | solution.py:28
  268.0 0.1 reshape.102
  268.1 0.1 slice_reduce_fusion
  268.2 0.1 reshape_squeeze.3
  268.3 0.1 add.66
  268.4 0.9 convert_reduce_fusion
  269.3 0.1 select_reduce_fusion
  269.4 0.1 copy.20
  269.5 0.1 sub.7
  269.7 0.1 copy.21
  269.8 0.1 min.18
  269.9 8.6 %gather_fusion = bf16[128,2,128,128]{3,2,1,0:T(8,128)(2,1)} fusion(bf16[2,64,128,128]{3,2,1,0:T(8,128)(2,1)} %param.7, s32[1024]{0:T(1024)S(1)} %pad_clamp_fusion), kind=kCustom, calls=%fused_computation | custom fusion | bytes 16777728 | tf_op jit(solution)/shard_map/jit(_take)/gather | solution.py:48
  278.5 0.0 all-to-all-done
  278.5 14.6 %reshape.91 = bf16[128,2,128,128]{3,2,1,0:T(8,128)(2,1)} reshape(bf16[64,2,32768]{2,1,0:T(2,128)(2,1)} %all-to-all-done) | data formatting | bytes 16777216 | tf_op jit(solution)/shard_map/reshape | solution.py:47
  293.1 8.2 %fusion = f32[128,128,128,1]{2,1,3,0:T(8,128)S(1)} fusion(bf16[128,2,128,128]{3,2,1,0:T(8,128)(2,1)} %reshape.91, bf16[128,2,128,128]{3,2,1,0:T(8,128)(2,1)} %gather_fusion, pred[128]{0:T(512)(128)(4,1)S(1)} %compare_and_fusion), kind=kOutput, calls=%fused_computation.3 | convolution fusion | flops 1077936128 | bytes 25165952 | tf_op jit(solution)/shard_map/tnij,ntjk->nik/dot_general | solution.py:49
  301.3 9.7 %copy.41 = f32[16,8,128,128]{3,1,2,0:T(8,128)} copy(f32[16,8,128,128]{3,2,1,0:T(8,128)S(1)} %bitcast.38) | data formatting | bytes 16777216
  311.1 9.0 %copy.24 = f32[16384,128]{1,0:T(8,128)} copy(f32[16384,128]{0,1:T(8,128)} %bitcast.40) | data formatting | bytes 16777216 | tf_op jit(solution)/shard_map/dot_general | solution.py:53
  320.1 10.5 %fusion.15 = f32[64,128,128]{2,0,1:T(8,128)} fusion(f32[128,128,128]{2,1,0:T(8,128)} %bitcast.39, s32[128]{0:T(128)S(1)} %sub.7), kind=kOutput, calls=%fused_computation.25 | convolution fusion | flops 1610620928 | bytes 12583424 | tf_op jit(solution)/shard_map/dot_general | solution.py:53
  330.6 78.5 %all-reduce.1 = bf16[64,128,128]{2,0,1:T(8,128)(2,1)} all-reduce(f32[64,128,128]{2,0,1:T(8,128)} %fusion.15), channel_id=1, replica_groups=mesh['term'=4,'sector'=64] {'term'}, use_global_device_ids=true, to_apply=%region_3.4 | all-reduce | flops 1048576 | bytes 6291456 | tf_op jit(solution)/shard_map/psum | solution.py:59
  409.1 1.1 dynamic-slice_convert_fusion
  410.2 1.1 copy.25
  (12 shorter events, 0.1 us)
Async XLA Ops:
  0.0 1.6 copy-start
  36.3 13.5 %copy-start.2 = (s32[64,1]{0,1:T(1,128)S(1)}, s32[64,1]{0,1:T(1,128)}, u32[]{:S(2)}) copy-start(s32[64,1]{0,1:T(1,128)} %param.8) | copy-start | bytes 772
  36.3 13.5 %copy-start.3 = (s32[64,1]{0,1:T(1,128)S(1)}, s32[64,1]{0,1:T(1,128)}, u32[]{:S(2)}) copy-start(s32[64,1]{0,1:T(1,128)} %param.9) | copy-start | bytes 772
  36.3 242.2 %all-to-all-start = ((bf16[64,2,32768]{2,1,0:T(2,128)(2,1)}), bf16[64,2,32768]{2,1,0:T(2,128)(2,1)}, u32[]{:S(2)}, u32[]{:S(2)}) async-start(bf16[64,2,32768]{2,1,0:T(2,128)(2,1)} %reshape.90), calls=%async_computation | async-start | bytes 16777216 | tf_op jit(solution)/shard_map/all_to_all | solution.py:44
  320.1 91.2 %copy-start.1 = (bf16[64,128,128]{2,1,0:T(8,128)(2,1)S(1)}, bf16[64,128,128]{2,1,0:T(8,128)(2,1)}, u32[]{:S(2)}) copy-start(bf16[64,128,128]{2,1,0:T(8,128)(2,1)} %param.5) | copy-start | bytes 6291460
where the time goes:
time: 413 us; the launch traced here: 411 us
  blocking collectives  297 us (72%)
  local copies, waits for them, and re-layouts  65.4 us (16%)
  matrix products  32.9 us (8%)
  starting transfers between devices  13.5 us (3%)
    all_gather x1, blocking collectives, local(): lax.all_gather(jnp.concatenate([owner_map, left_local], axis=1), 'sector'...  218 us
    psum x1, blocking collectives, local(): total = lax.psum(partial_sum, 'term')  78.5 us
    reshape x1, local copies, waits for them, and re-layouts, local(): arrived = arrived.reshape(slots, terms_dev, width, width)  14.6 us
    reshape x1, local copies, waits for them, and re-layouts, local(): packed.reshape(n_sector, capacity, -1)  14.1 us
    all_to_all x1, starting transfers between devices, local(): lax.all_to_all(packed.reshape(n_sector, capacity, -1), 'sector', split_ax...  13.5 us
    dot_general x1, matrix products, local(): jnp.dot(collect, images.reshape(slots, -1), precision=lax.Precision.HIGHE...  10.5 us
    unnamed x10, local copies, waits for them, and re-layouts  9.9 us
    dot_general x1, local copies, waits for them, and re-layouts, local(): jnp.dot(collect, images.reshape(slots, -1), precision=lax.Precision.HIGHE...  8.99 us
  transfers between devices with their start and end apart: 1, of which 0 were waited for; matrix products, arithmetic and copies ran while one was open for 3% of the time, Pallas kernels for 0%

commit v1 on v0

--- a/solution.py
+++ b/solution.py
@@ -25,8 +25,14 @@
     packer = (lax.broadcasted_iota(jnp.int32, (slots, sec_dev), 0) == slot_id[None, :]).astype(
         jnp.bfloat16
     )
-    routes_all = lax.all_gather(
-        jnp.concatenate([owner_map, left_local], axis=1), "sector", axis=0, tiled=True
+    routes_all = jnp.concatenate(
+        lax.all_to_all(
+            jnp.stack([jnp.concatenate([owner_map, left_local], axis=1)] * lax.axis_size("sector")),
+            "sector",
+            0,
+            0,
+        ),
+        axis=0,
     )
     all_owners = routes_all[:, 0].reshape(n_sector, sec_dev)
     all_local = routes_all[:, 1].reshape(n_sector, sec_dev)

time: 413 us -> 382 us (0.925)
  blocking collectives: 297 us -> 79.8 us
  waiting for transfers between devices: 0.01 us -> 174 us
  starting transfers between devices: 13.5 us -> 23.6 us
    all_gather x1 -> x0, blocking collectives: 218 us -> none  [local(): lax.all_gather(jnp.concatenate([owner_map, left_local], axis=1), 'sector'...]
    all_to_all x1, waiting for transfers between devices: 0.01 us -> 174 us  [local(): lax.all_to_all(packed.reshape(n_sector, capacity, -1), 'sector', split_ax...]
    all_to_all x0 -> x1, starting transfers between devices: none -> 13.1 us  [local(): lax.all_to_all(jnp.stack([jnp.concatenate([owner_map, left_local], axis=1...]
    unnamed x10 -> x8, local copies, waits for them, and re-layouts: 9.9 us -> 10.6 us
  transfers between devices with their start and end apart: 1 -> 2, of which waited for: 0 -> 1; matrix products, arithmetic and copies ran while one was open for 3% -> 13% of each run, Pallas kernels for 0% -> 0%
where the time goes in v1:
time: 382 us; the launch traced here: 381 us
  waiting for transfers between devices  174 us (46%)
  blocking collectives  79.8 us (21%)
  local copies, waits for them, and re-layouts  66.7 us (17%)
  matrix products  32.8 us (9%)
  starting transfers between devices  23.6 us (6%)
  other arithmetic  3.98 us (1%)
    all_to_all x1, waiting for transfers between devices, local(): lax.all_to_all(packed.reshape(n_sector, capacity, -1), 'sector', split_ax...  174 us
    psum x1, blocking collectives, local(): total = lax.psum(partial_sum, 'term')  79.8 us
    reshape x1, local copies, waits for them, and re-layouts, local(): arrived = arrived.reshape(slots, terms_dev, width, width)  14.6 us
    reshape x1, local copies, waits for them, and re-layouts, local(): packed.reshape(n_sector, capacity, -1)  14.1 us
    all_to_all x1, starting transfers between devices, local(): lax.all_to_all(jnp.stack([jnp.concatenate([owner_map, left_local], axis=1...  13.1 us
    unnamed x8, local copies, waits for them, and re-layouts  10.6 us
    all_to_all x1, starting transfers between devices, local(): lax.all_to_all(packed.reshape(n_sector, capacity, -1), 'sector', split_ax...  10.5 us
    dot_general x1, matrix products, local(): jnp.dot(collect, images.reshape(slots, -1), precision=lax.Precision.HIGHE...  10.5 us
  transfers between devices with their start and end apart: 2, of which 1 were waited for; matrix products, arithmetic and copies ran while one was open for 13% of the time, Pallas kernels for 0%

profile of v1, /device:TPU:1, one launch (start us, length us, event | category | flops | bytes accessed | tf_op | source)
XLA Modules:
  0.0 381.1 jit_solution(13319439794850033618)
XLA Ops:
  0.0 0.8 pad_add_fusion
  0.9 0.7 reshape.122
  1.6 13.1 %all-to-all-start = ((s32[64,1,128]{2,1,0:T(1,128)}), s32[64,1,128]{2,1,0:T(1,128)S(1)}, u32[]{:S(2)}, u32[]{:S(2)}) async-start(s32[64,1,128]{2,1,0:T(1,128)} %reshape.122), calls=%async_computation | async-start | bytes 65536 | tf_op jit(solution)/shard_map/all_to_all | solution.py:29
  14.7 0.8 convert_reduce_fusion.1
  15.6 0.7 multiply_add_fusion
  16.2 5.4 %convert_bitcast_fusion = bf16[64,2,128,128]{2,3,1,0:T(8,128)(2,1)} fusion(bf16[2,64,128,128]{3,2,1,0:T(8,128)(2,1)} %param.6, bf16[64,128,128]{2,1,0:T(8,128)(2,1)S(1)} %copy-done), kind=kOutput, calls=%fused_computation.12 | convolution fusion | flops 538968064 | bytes 10485760 | tf_op jit(solution)/shard_map/sij,tsjk->stik/dot_general | solution.py:44
  21.6 6.3 %copy.27 = bf16[64,2,128,128]{3,2,1,0:T(8,128)(2,1)} copy(bf16[64,2,128,128]{2,3,1,0:T(8,128)(2,1)} %convert_bitcast_fusion) | data formatting | bytes 8388608 | tf_op jit(solution)/shard_map/convert_element_type | solution.py:46
  28.0 8.8 %convolution_convert_fusion = bf16[128,32768]{1,0:T(8,128)(2,1)} fusion(bf16[8,8,256,128]{3,2,1,0:T(8,128)(2,1)} %bitcast.42, s32[64]{0:T(128)S(1)} %multiply_add_fusion), kind=kOutput, calls=%fused_computation.1 | convolution fusion | flops 541073408 | bytes 12583168 | tf_op jit(solution)/shard_map/dot_general | solution.py:47
  36.7 14.1 %reshape.96 = bf16[64,2,32768]{2,1,0:T(2,128)(2,1)} reshape(bf16[128,32768]{1,0:T(8,128)(2,1)} %convolution_convert_fusion) | data formatting | bytes 16777216 | tf_op jit(solution)/shard_map/reshape | solution.py:51
  50.9 10.5 %all-to-all-start.1 = ((bf16[64,2,32768]{2,1,0:T(2,128)(2,1)}), bf16[64,2,32768]{2,1,0:T(2,128)(2,1)}, u32[]{:S(2)}, u32[]{:S(2)}) async-start(bf16[64,2,32768]{2,1,0:T(2,128)(2,1)} %reshape.96), calls=%async_computation.1 | async-start | bytes 16777216 | tf_op jit(solution)/shard_map/all_to_all | solution.py:50
  61.4 0.5 broadcast.110
  61.9 0.7 reduce.8
  62.7 0.1 reshape.123
  62.8 0.1 reshape.94
  62.9 0.1 slice_reduce_fusion
  63.0 0.1 reshape_squeeze.3
  63.1 0.7 convert_reduce_fusion
  63.8 0.1 select_reduce_fusion
  64.0 0.1 copy.24
  64.0 0.1 sub.7
  64.2 0.1 copy.25
  64.3 0.1 min.18
  64.5 8.6 %gather_fusion = bf16[128,2,128,128]{3,2,1,0:T(8,128)(2,1)} fusion(bf16[2,64,128,128]{3,2,1,0:T(8,128)(2,1)} %param.7, s32[1024]{0:T(1024)S(1)} %pad_clamp_fusion), kind=kCustom, calls=%fused_computation | custom fusion | bytes 16777728 | tf_op jit(solution)/shard_map/jit(_take)/gather | solution.py:54
  73.0 174.1 %all-to-all-done.1 = bf16[64,2,32768]{2,1,0:T(2,128)(2,1)} async-done(((bf16[64,2,32768]{2,1,0:T(2,128)(2,1)}), bf16[64,2,32768]{2,1,0:T(2,128)(2,1)}, u32[]{:S(2)}, u32[]{:S(2)}) %all-to-all-start.1) | async-done | bytes 8388640 | tf_op jit(solution)/shard_map/all_to_all | solution.py:50
  247.1 14.6 %reshape.97 = bf16[128,2,128,128]{3,2,1,0:T(8,128)(2,1)} reshape(bf16[64,2,32768]{2,1,0:T(2,128)(2,1)} %all-to-all-done.1) | data formatting | bytes 16777216 | tf_op jit(solution)/shard_map/reshape | solution.py:53
  261.7 8.2 %fusion = f32[128,128,128,1]{2,1,3,0:T(8,128)S(1)} fusion(bf16[128,2,128,128]{3,2,1,0:T(8,128)(2,1)} %reshape.97, bf16[128,2,128,128]{3,2,1,0:T(8,128)(2,1)} %gather_fusion, pred[128]{0:T(512)(128)(4,1)S(1)} %compare_and_fusion), kind=kOutput, calls=%fused_computation.3 | convolution fusion | flops 1077936128 | bytes 25165952 | tf_op jit(solution)/shard_map/tnij,ntjk->nik/dot_general | solution.py:55
  269.9 9.7 %copy.45 = f32[16,8,128,128]{3,1,2,0:T(8,128)} copy(f32[16,8,128,128]{3,2,1,0:T(8,128)S(1)} %bitcast.39) | data formatting | bytes 16777216
  279.7 9.0 %copy.28 = f32[16384,128]{1,0:T(8,128)} copy(f32[16384,128]{0,1:T(8,128)} %bitcast.41) | data formatting | bytes 16777216 | tf_op jit(solution)/shard_map/dot_general | solution.py:59
  288.7 10.5 %fusion.15 = f32[64,128,128]{2,0,1:T(8,128)} fusion(f32[128,128,128]{2,1,0:T(8,128)} %bitcast.40, s32[128]{0:T(128)S(1)} %sub.7), kind=kOutput, calls=%fused_computation.25 | convolution fusion | flops 1610620928 | bytes 12583424 | tf_op jit(solution)/shard_map/dot_general | solution.py:59
  299.1 79.8 %all-reduce.1 = bf16[64,128,128]{2,0,1:T(8,128)(2,1)} all-reduce(f32[64,128,128]{2,0,1:T(8,128)} %fusion.15), channel_id=1, replica_groups=mesh['term'=4,'sector'=64] {'term'}, use_global_device_ids=true, to_apply=%region_3.4 | all-reduce | flops 1048576 | bytes 6291456 | tf_op jit(solution)/shard_map/psum | solution.py:65
  378.9 1.1 dynamic-slice_convert_fusion
  380.0 1.1 copy.29
  (14 shorter events, 0.2 us)
Async XLA Ops:
  0.0 16.2 %copy-start = (bf16[64,128,128]{2,1,0:T(8,128)(2,1)S(1)}, bf16[64,128,128]{2,1,0:T(8,128)(2,1)}, u32[]{:S(2)}) copy-start(bf16[64,128,128]{2,1,0:T(8,128)(2,1)} %param.5) | copy-start | bytes 6291460
  1.6 49.3 %all-to-all-start = ((s32[64,1,128]{2,1,0:T(1,128)}), s32[64,1,128]{2,1,0:T(1,128)S(1)}, u32[]{:S(2)}, u32[]{:S(2)}) async-start(s32[64,1,128]{2,1,0:T(1,128)} %reshape.122), calls=%async_computation | async-start | bytes 65536 | tf_op jit(solution)/shard_map/all_to_all | solution.py:29
  50.9 196.2 %all-to-all-start.1 = ((bf16[64,2,32768]{2,1,0:T(2,128)(2,1)}), bf16[64,2,32768]{2,1,0:T(2,128)(2,1)}, u32[]{:S(2)}, u32[]{:S(2)}) async-start(bf16[64,2,32768]{2,1,0:T(2,128)(2,1)} %reshape.96), calls=%async_computation.1 | async-start | bytes 16777216 | tf_op jit(solution)/shard_map/all_to_all | solution.py:50
  288.7 92.5 %copy-start.1 = (bf16[64,128,128]{2,1,0:T(8,128)(2,1)S(1)}, bf16[64,128,128]{2,1,0:T(8,128)(2,1)}, u32[]{:S(2)}) copy-start(bf16[64,128,128]{2,1,0:T(8,128)(2,1)} %param.5) | copy-start | bytes 6291460
